TPU v7x, 512 devices: a whole 4x8x8 slice. The times are simulated.
512 devices in a mesh: dp: 4 (over x), seq: 16 (over z, core), tensor: 8 (over y).
Axes of the slice: x: 4, y: 8, z: 8, core: 2. Of those that a mesh axis runs over, the one named last changes fastest.
Arguments:
- hidden: bfloat16 [8192, 8192], P(('dp', 'seq'), 'tensor'), may hold values from -6 to 6
- queries: bfloat16 [8192, 8192], P(('dp', 'seq'), 'tensor'), may hold values from -14 to 14
- kv_weight: bfloat16 [8192, 2048], P('seq', 'tensor'), may hold values from -0.0625 to 0.0625
- parents: int32 [4, 16], P('dp'), may hold values from -1 to 14, as said below
- out_grad: bfloat16 [8192, 8192], P(('dp', 'seq'), 'tensor'), may hold values from -6 to 6
Outputs:
- attended: bfloat16 [8192, 8192], P(('dp', 'seq'), 'tensor')
- query_grad: float32 [8192, 8192], P(('dp', 'seq'), 'tensor')
- weight_grad: float32 [8192, 2048], P('seq', 'tensor')
Inputs may be any that keep to these rules, and one draw needn't show every extreme that they name: parents[g, n] is -1 where node block n begins a new tree of group g (always for n = 0), else an earlier node block of the same group; the last node block of every group has parent 16 - 2.
All inputs are finite; a program needn't handle non-finite values.
Results may differ from a plain program's by a relative error of at most 0.012.
The roundings to bfloat16 on the way count: a program that leaves them out, or rounds other values in their place, can miss the bound.
Values may be sent and summed in bfloat16 or wider, within the bound.
No kernel may reach another device: no remote copies, remote signals or barrier semaphores. Data moves between devices by JAX's collectives and lax.ppermute only.
A program may use at most 64 MiB of HBM per device.

v0:
```python
import math
import jax
import jax.numpy as jnp
from jax import lax
from jax.sharding import PartitionSpec as P

HD = 128


def attend_block(query_blk, grad_blk, keys_head, values_head, visible):
    inv_root = 1.0 / math.sqrt(query_blk.shape[-1])
    scores = (
        jnp.einsum("thd,jd->htj", query_blk, keys_head, preferred_element_type=jnp.float32)
        * inv_root
    )
    scores = jnp.where(visible[None], scores, -jnp.inf)
    row_top = jnp.max(scores, axis=-1, keepdims=True)
    expons = jnp.exp(scores - row_top)
    probs_f = expons / jnp.sum(expons, axis=-1, keepdims=True)
    weights = probs_f.astype(jnp.bfloat16)
    mixed_f = jnp.einsum("htj,jd->thd", weights, values_head, preferred_element_type=jnp.float32)
    prob_grad = jnp.einsum("thd,jd->htj", grad_blk, values_head, preferred_element_type=jnp.float32)
    inner_sum = jnp.transpose(jnp.sum(grad_blk.astype(jnp.float32) * mixed_f, axis=-1), (1, 0))
    score_grad = (probs_f * (prob_grad - inner_sum[:, :, None]) * inv_root).astype(jnp.bfloat16)
    query_grad = jnp.einsum(
        "htj,jd->thd", score_grad, keys_head, preferred_element_type=jnp.float32
    )
    key_grad = jnp.einsum("htj,thd->jd", score_grad, query_blk, preferred_element_type=jnp.float32)
    value_grad = jnp.einsum("htj,thd->jd", weights, grad_blk, preferred_element_type=jnp.float32)
    return (mixed_f.astype(jnp.bfloat16), query_grad, key_grad, value_grad)


def per_device(hidden, queries, kv_weight, parents, out_grad):
    tok_rows = queries.shape[0]
    head_size = HD
    kv_local = kv_weight.shape[1] // (2 * head_size)
    heads_local = queries.shape[1] // head_size
    heads_per = heads_local // kv_local
    block_heads = max(1, min(heads_per, 512 // tok_rows))
    block_count = heads_per // block_heads
    node_count = lax.axis_size("seq")
    my_node = lax.axis_index("seq")
    group_rows = tok_rows * node_count
    whole_rows = lax.all_gather(hidden, "tensor", axis=1, tiled=True)
    traded = lax.all_to_all(whole_rows, "seq", split_axis=1, concat_axis=0, tiled=True)
    partial_kv = jnp.dot(traded, kv_weight, preferred_element_type=jnp.float32)
    kv_all = lax.psum(partial_kv, "seq").astype(jnp.bfloat16)
    parent_list = parents[0]
    node_ids = jnp.arange(node_count, dtype=jnp.int32)

    def follow(step_index, state_pair):
        current, marked = state_pair
        marked = jnp.maximum(marked, (node_ids == current).astype(jnp.int32))
        current = jnp.where(current >= 0, parent_list[jnp.maximum(current, 0)], -1)
        return (current, marked)

    start_pair = (parent_list[my_node], jnp.zeros((node_count,), jnp.int32))
    final_pair = lax.fori_loop(0, node_count, follow, start_pair)
    key_above = jnp.broadcast_to(final_pair[1][:, None] > 0, (node_count, tok_rows)).reshape(
        group_rows
    )
    key_node = jnp.arange(group_rows, dtype=jnp.int32) // tok_rows
    key_pos = jnp.arange(group_rows, dtype=jnp.int32) % tok_rows
    query_pos = jnp.arange(tok_rows, dtype=jnp.int32)
    visible = key_above[None, :] | (key_node == my_node)[None, :] & (
        key_pos[None, :] <= query_pos[:, None]
    )
    kv_heads = kv_all.reshape(group_rows, kv_local, 2, head_size).transpose(1, 0, 2, 3)
    query_split = queries.reshape(
        tok_rows, kv_local, block_count, block_heads, head_size
    ).transpose(1, 2, 0, 3, 4)
    grad_split = out_grad.reshape(
        tok_rows, kv_local, block_count, block_heads, head_size
    ).transpose(1, 2, 0, 3, 4)

    def per_head(packed):
        query_head, grad_head, head_kv = packed
        keys_head = head_kv[:, 0, :]
        values_head = head_kv[:, 1, :]

        def per_part(running, block_pair):
            mixed_blk, qgrad_blk, key_grad, value_grad = attend_block(
                block_pair[0], block_pair[1], keys_head, values_head, visible
            )
            return ((running[0] + key_grad, running[1] + value_grad), (mixed_blk, qgrad_blk))

        zero_grad = jnp.zeros((group_rows, head_size), jnp.float32)
        sums_pair, outputs = lax.scan(per_part, (zero_grad, zero_grad), (query_head, grad_head))
        return (outputs[0], outputs[1], jnp.stack([sums_pair[0], sums_pair[1]], axis=1))

    mixed_all, qgrad_all, kv_terms = lax.map(per_head, (query_split, grad_split, kv_heads))
    attended = mixed_all.transpose(2, 0, 1, 3, 4).reshape(tok_rows, heads_local * head_size)
    query_grad = qgrad_all.transpose(2, 0, 1, 3, 4).reshape(tok_rows, heads_local * head_size)
    kv_terms = kv_terms.transpose(1, 0, 2, 3).reshape(group_rows, kv_local * 2 * head_size)
    kv_grads = lax.psum(kv_terms.astype(jnp.bfloat16), "seq")
    local_weight = lax.dot_general(
        traded, kv_grads, (((0,), (0,)), ((), ())), preferred_element_type=jnp.float32
    )
    weight_grad = lax.psum(local_weight * (1.0 / (lax.axis_size("dp") * node_count)), "dp")
    return (attended, query_grad, weight_grad)


def solution(mesh):
    placed = (
        P(("dp", "seq"), "tensor"),
        P(("dp", "seq"), "tensor"),
        P("seq", "tensor"),
        P("dp", None),
        P(("dp", "seq"), "tensor"),
    )
    return jax.shard_map(
        per_device,
        mesh=mesh,
        in_specs=placed,
        out_specs=(P(("dp", "seq"), "tensor"), P(("dp", "seq"), "tensor"), P("seq", "tensor")),
        check_vma=False,
    )
```

profile of v0, /device:TPU:8, one launch (start us, length us, event | category | flops | bytes accessed | tf_op | source)
XLA Modules:
  0.0 414.3 jit_solution(17990220807136559389)
XLA Ops:
  7.2 1.8 copy.37
  9.1 1.1 copy.36
  10.3 1.8 copy.40
  12.1 1.3 constant_dynamic-slice_fusion.1
  13.4 45.1 %all-gather.2.cloned.1.call-done = bf16[128,8192]{0,1:T(8,128)(2,1)} async-done(((bf16[128,1024]{0,1:T(8,128)(2,1)}), bf16[128,8192]{0,1:T(8,128)(2,1)}) %all-gather.2.cloned.1.call-update) | async-done | bytes 2097168 | tf_op jit(solution)/shard_map/all_gather | solution.py:44
  58.4 7.5 %all-to-all-start = ((bf16[128,16,512]{0,2,1:T(8,128)(2,1)}), bf16[128,16,512]{0,2,1:T(8,128)(2,1)S(1)}, u32[]{:S(2)}, u32[]{:S(2)}) async-start(bf16[128,16,512]{0,2,1:T(8,128)(2,1)} %bitcast.163), calls=%async_computation | async-start | bytes 4194304 | tf_op jit(solution)/shard_map/all_to_all | solution.py:45
  66.0 40.3 %while.42 = (s32[]{:T(128)}, s32[]{:T(128)}, s32[16]{0:T(128)S(1)}, s32[16]{0:T(128)S(1)}, s32[]{:T(128)}, /*index=5*/s32[]{:T(128)}, s32[]{:T(128)}) while((s32[]{:T(128)}, s32[]{:T(128)}, s32[16]{0:T(128)S(1)}, s32[16]{0:T(128)S(1)}, s32[]{:T(128)}, /*index=5*/s32[]{:T(128)}, s32[]{:T(128)}) %tuple.73), condition=%wide.region_2.3_spmd.clone, body=%wide.region_1.2_spmd.clone.sunk | while | flops 70 | bytes 273 | solution.py:58
  106.4 8.8 %all-to-all-done = bf16[128,16,512]{0,2,1:T(8,128)(2,1)S(1)} async-done(((bf16[128,16,512]{0,2,1:T(8,128)(2,1)}), bf16[128,16,512]{0,2,1:T(8,128)(2,1)S(1)}, u32[]{:S(2)}, u32[]{:S(2)}) %all-to-all-start) | async-done | bytes 2097184 | tf_op jit(solution)/shard_map/all_to_all | solution.py:45
  115.2 1.3 copy-done.7
  116.5 2.9 copy.38
  119.4 2.0 fusion.48
  121.4 60.2 %all-reduce.7 = bf16[2048,256]{1,0:T(8,128)(2,1)} all-reduce(f32[2048,256]{1,0:T(8,128)} %fusion.48), channel_id=1, replica_groups=mesh['dp'=4,'seq'=16,'tensor'=8] {'seq'}, use_global_device_ids=true, to_apply=%region_0.0 | all-reduce | flops 524288 | bytes 3145728 | tf_op jit(solution)/shard_map/psum | solution.py:47
  181.6 2.2 squeeze.41
  183.8 3.2 fusion.47
  187.0 1.8 copy.57
  188.9 39.9 %while.43 = (s32[]{:T(128)}, f32[2048,128]{1,0:T(8,128)}, f32[2048,128]{1,0:T(8,128)}, bf16[2,128,4,128]{3,1,2,0:T(8,128)(2,1)}, f32[2,128,4,128]{3,1,2,0:T(8,12...) while((s32[]{:T(128)}, f32[2048,128]{1,0:T(8,128)}, ...), condition=%wide.region_7.8_spmd.clone, body=%wide.region_3.7_spmd.clone.sunk | while | flops 1626342912 | bytes 79985504 | solution.py:88
  188.9 0.7 fusion.89
  189.8 1.9 fusion.91
  191.7 1.9 copy-done.2
  194.3 0.9 constant_dynamic-slice_fusion.3
  195.4 1.8 multiply_reduce_fusion.2
  197.2 4.5 %fusion.93 = bf16[4,128,2048]{2,1,0:T(8,128)(2,1)} fusion(f32[4,128]{1,0:T(4,128)S(1)} %bitcast.169, f32[4,128,2048]{2,1,0:T(8,128)} %copy-done.2, f32[4,128]{1,0:T(4,128)} %copy-done.11, bf16[2048,128]{0,1:T(8,128)(2,1)} %get-tuple-element.411, bf16[1,128,4,128]{1,3,2,0:T(8,128)(2,1)S(1)} %constant_dynamic-slice_fusion.3), kind=kOutput, calls=%fused_computation.9.clone.1 | convolution fusion | flops 273678336 | bytes 6950912 | tf_op jit(solution)/shard_map/while/body/eval_jaxpr/while/body/eval_jaxpr/thd,jd->htj/dot_general | solution.py:22
  201.8 3.5 fusion.94
  205.3 0.7 fusion.96
  206.1 1.0 fusion.95
  207.1 0.9 copy-done.4
  208.1 0.7 bitcast_dynamic-update-slice_fusion.2
  208.7 0.7 fusion.89
  209.7 1.9 fusion.91
  211.6 1.9 copy-done.2
  214.2 0.9 constant_dynamic-slice_fusion.3
  215.2 1.8 multiply_reduce_fusion.2
  217.1 4.5 %fusion.93 = bf16[4,128,2048]{2,1,0:T(8,128)(2,1)} fusion(f32[4,128]{1,0:T(4,128)S(1)} %bitcast.169, f32[4,128,2048]{2,1,0:T(8,128)} %copy-done.2, f32[4,128]{1,0:T(4,128)} %copy-done.11, bf16[2048,128]{0,1:T(8,128)(2,1)} %get-tuple-element.411, bf16[1,128,4,128]{1,3,2,0:T(8,128)(2,1)S(1)} %constant_dynamic-slice_fusion.3), kind=kOutput, calls=%fused_computation.9.clone.1 | convolution fusion | flops 273678336 | bytes 6950912 | tf_op jit(solution)/shard_map/while/body/eval_jaxpr/while/body/eval_jaxpr/thd,jd->htj/dot_general | solution.py:22
  221.6 3.8 fusion.94
  225.4 0.7 fusion.96
  226.1 1.0 fusion.95
  227.2 0.9 copy-done.4
  228.1 0.7 bitcast_dynamic-update-slice_fusion.2
  228.8 1.6 copy.47
  230.4 1.4 copy.46
  231.8 1.1 pad_maximum_fusion
  233.0 116.3 %all-reduce.4.cloned.1.call-done = bf16[2048,256]{0,1:T(8,128)(2,1)} async-done(((bf16[2048,256]{0,1:T(8,128)(2,1)}), bf16[2048,256]{0,1:T(8,128)(2,1)}) %all-reduce.4.cloned.1.call-update) | async-done | bytes 1048592 | tf_op jit(solution)/shard_map/psum | solution.py:95
  349.3 2.7 fusion.37
  352.5 1.0 reshape.59
  353.5 1.2 copy.44
  354.6 0.9 reshape.58
  355.5 50.2 %all-reduce.6.cloned.1.call-done = f32[512,256]{0,1:T(8,128)} async-done(((f32[512,256]{0,1:T(8,128)}), f32[512,256]{0,1:T(8,128)}) %all-reduce.6.cloned.1.call-update) | async-done | bytes 524304 | tf_op jit(solution)/shard_map/psum | solution.py:99
  405.7 2.0 copy.48
  (90 shorter events, 12.3 us)
Async XLA Ops:
  7.2 112.2 %copy-start = (bf16[512,256]{1,0:T(8,128)(2,1)S(1)}, bf16[512,256]{1,0:T(8,128)(2,1)}, u32[]{:S(2)}) copy-start(bf16[512,256]{1,0:T(8,128)(2,1)} %param.11) | copy-start | bytes 786436
  7.2 58.8 %copy-start.12 = (s32[1,16]{1,0:T(1,128)S(1)}, s32[1,16]{1,0:T(1,128)}, u32[]{:S(2)}) copy-start(s32[1,16]{1,0:T(1,128)} %param.12) | copy-start | bytes 196
  7.2 51.3 %all-gather.2.cloned.1.call-start = ((), (), s32[]{:S(2)}) async-start(), calls=%async_computation.1 | async-start | bytes 2359296 | tf_op jit(solution)/shard_map/all_gather | solution.py:44
  58.4 56.7 %all-to-all-start = ((bf16[128,16,512]{0,2,1:T(8,128)(2,1)}), bf16[128,16,512]{0,2,1:T(8,128)(2,1)S(1)}, u32[]{:S(2)}, u32[]{:S(2)}) async-start(bf16[128,16,512]{0,2,1:T(8,128)(2,1)} %bitcast.163), calls=%async_computation | async-start | bytes 4194304 | tf_op jit(solution)/shard_map/all_to_all | solution.py:45
  65.9 283.4 %all-reduce.4.cloned.1.call-start = ((), (), s32[]{:S(2)}) async-start(), calls=%async_computation.2 | async-start | bytes 2097152 | tf_op jit(solution)/shard_map/psum | solution.py:95
  115.2 1.3 copy-start.7
  119.4 62.2 %copy-start.5 = (bf16[16,128,512]{2,1,0:T(8,128)(2,1)}, bf16[16,128,512]{2,1,0:T(8,128)(2,1)S(1)}, u32[]{:S(2)}) copy-start(bf16[16,128,512]{2,1,0:T(8,128)(2,1)S(1)} %copy.38) | copy-start | bytes 6291460
  191.7 2.0 copy-start.2
  191.7 2.6 copy-start.11
  201.8 3.6 copy-start.1
  201.8 3.6 copy-start.8
  201.8 4.3 %copy-start.3 = (f32[2048,128]{1,0:T(8,128)S(1)}, f32[2048,128]{1,0:T(8,128)}, u32[]{:S(2)}) copy-start(f32[2048,128]{1,0:T(8,128)} %get-tuple-element.391) | copy-start | bytes 3145732 | tf_op jit(solution)/shard_map/while/body/eval_jaxpr/while
  206.0 2.0 copy-start.9
  207.1 1.0 copy-start.4
  211.5 2.0 copy-start.2
  211.5 2.6 copy-start.11
  221.6 3.8 copy-start.1
  221.6 3.8 copy-start.8
  221.6 4.5 %copy-start.3 = (f32[2048,128]{1,0:T(8,128)S(1)}, f32[2048,128]{1,0:T(8,128)}, u32[]{:S(2)}) copy-start(f32[2048,128]{1,0:T(8,128)} %get-tuple-element.391) | copy-start | bytes 3145732 | tf_op jit(solution)/shard_map/while/body/eval_jaxpr/while
  226.1 2.0 copy-start.9
  227.2 1.0 copy-start.4
  228.8 120.5 %copy-start.6 = (bf16[16,128,512]{2,1,0:T(8,128)(2,1)S(1)}, bf16[16,128,512]{2,1,0:T(8,128)(2,1)}, u32[]{:S(2)}) copy-start(bf16[16,128,512]{2,1,0:T(8,128)(2,1)} %copy-done.5) | copy-start | bytes 6291460
  232.9 119.2 %copy-start.10 = (f32[2,128,4,128]{3,1,2,0:T(8,128)S(1)}, f32[2,128,4,128]{3,1,2,0:T(8,128)}, u32[]{:S(2)}) copy-start(f32[2,128,4,128]{3,1,2,0:T(8,128)} %get-tuple-element.111) | copy-start | bytes 1572868
  232.9 172.8 %all-reduce.6.cloned.1.call-start = ((), (), s32[]{:S(2)}) async-start(), calls=%async_computation.3 | async-start | bytes 1048576 | tf_op jit(solution)/shard_map/psum | solution.py:99
Sparse Core Ops, SparseCore 0:
  10.7 47.7 all-gather.1
  233.1 116.2 all-reduce.3
  352.2 53.4 all-reduce.5
where the time goes:
time: 415 us; the launch traced here: 414 us
  waiting for transfers between devices  220 us (53%)
  blocking collectives  60.2 us (15%)
  local copies, waits for them, and re-layouts  44.7 us (11%)
  loops' own time  30.9 us (7%)
  matrix products  29.8 us (7%)
  between operations  13.9 us (3%)
  starting transfers between devices  7.6 us (2%)
  other arithmetic  6.75 us (2%)
    psum x1, waiting for transfers between devices, per_device(): kv_grads = lax.psum(kv_terms.astype(jnp.bfloat16), 'seq')  116 us
    psum x1, blocking collectives, per_device(): kv_all = lax.psum(partial_kv, 'seq').astype(jnp.bfloat16)  60.2 us
    psum x1, waiting for transfers between devices, per_device(): lax.psum(local_weight * (1.0 / (lax.axis_size('dp') * node_count)), 'dp')  50.2 us
    all_gather x1, waiting for transfers between devices, per_device(): whole_rows = lax.all_gather(hidden, 'tensor', axis=1, tiled=True)  45.1 us
    another operation x1, loops' own time, per_device(): final_pair = lax.fori_loop(0, node_count, follow, start_pair)  30.7 us
    unnamed x18, local copies, waits for them, and re-layouts  10 us
    dynamic_slice x16, local copies, waits for them, and re-layouts, follow(): current = jnp.where(current >= 0, parent_list[jnp.maximum(current, 0)], -1)  9.39 us
    dot_general x2, matrix products, attend_block(): jnp.einsum('thd,jd->htj', grad_blk, values_head, preferred_element_type=j...  9.07 us
  transfers between devices with their start and end apart: 4, of which 4 were waited for; matrix products, arithmetic and copies ran while one was open for 4% of the time, Pallas kernels for 0%

commit v1 on v0

--- a/solution.py
+++ b/solution.py
@@ -96,7 +96,9 @@
     local_weight = lax.dot_general(
         traded, kv_grads, (((0,), (0,)), ((), ())), preferred_element_type=jnp.float32
     )
-    weight_grad = lax.psum(local_weight * (1.0 / (lax.axis_size("dp") * node_count)), "dp")
+    weight_grad = jnp.sum(
+        lax.all_gather(local_weight * (1.0 / (lax.axis_size("dp") * node_count)), "dp"), axis=0
+    )
     return (attended, query_grad, weight_grad)
 
 

time: 415 us -> 401 us (0.966)
  the two profiles are of different devices: /device:TPU:8 before, /device:TPU:1 now
where the time goes in v1:
time: 401 us; the launch traced here: 400 us
  waiting for transfers between devices  202 us (50%)
  blocking collectives  56.6 us (14%)
  local copies, waits for them, and re-layouts  46.3 us (12%)
  loops' own time  30.9 us (8%)
  matrix products  29.8 us (7%)
  between operations  13.9 us (3%)
  starting transfers between devices  12.5 us (3%)
  other arithmetic  7.99 us (2%)
    psum x1, waiting for transfers between devices, per_device(): kv_grads = lax.psum(kv_terms.astype(jnp.bfloat16), 'seq')  119 us
    psum x1, blocking collectives, per_device(): kv_all = lax.psum(partial_kv, 'seq').astype(jnp.bfloat16)  56.6 us
    all_gather x1, waiting for transfers between devices, per_device(): whole_rows = lax.all_gather(hidden, 'tensor', axis=1, tiled=True)  42 us
    all_gather x1, waiting for transfers between devices, per_device(): lax.all_gather(local_weight * (1.0 / (lax.axis_size('dp') * node_count)),...  32.5 us
    another operation x1, loops' own time, per_device(): final_pair = lax.fori_loop(0, node_count, follow, start_pair)  30.7 us
    all_to_all x1, starting transfers between devices, per_device(): lax.all_to_all(whole_rows, 'seq', split_axis=1, concat_axis=0, tiled=True)  12.2 us
    dynamic_slice x16, local copies, waits for them, and re-layouts, follow(): current = jnp.where(current >= 0, parent_list[jnp.maximum(current, 0)], -1)  9.39 us
    dot_general x2, matrix products, attend_block(): jnp.einsum('thd,jd->htj', grad_blk, values_head, preferred_element_type=j...  9.07 us
  transfers between devices with their start and end apart: 4, of which 4 were waited for; matrix products, arithmetic and copies ran while one was open for 4% of the time, Pallas kernels for 0%

profile of v1, /device:TPU:1, one launch (start us, length us, event | category | flops | bytes accessed | tf_op | source)
XLA Modules:
  0.0 400.3 jit_solution(12857773980662832948)
XLA Ops:
  7.2 1.8 copy.51
  9.1 1.1 copy.50
  10.3 1.8 copy.54
  12.1 1.3 constant_dynamic-slice_fusion.1
  13.4 42.0 %all-gather.4.cloned.1.call-done = bf16[128,8192]{0,1:T(8,128)(2,1)} async-done(((bf16[128,1024]{0,1:T(8,128)(2,1)}), bf16[128,8192]{0,1:T(8,128)(2,1)}) %all-gather.4.cloned.1.call-update) | async-done | bytes 2097168 | tf_op jit(solution)/shard_map/all_gather | solution.py:44
  55.4 12.2 %all-to-all-start = ((bf16[128,16,512]{0,2,1:T(8,128)(2,1)}), bf16[128,16,512]{0,2,1:T(8,128)(2,1)S(1)}, u32[]{:S(2)}, u32[]{:S(2)}) async-start(bf16[128,16,512]{0,2,1:T(8,128)(2,1)} %bitcast.165), calls=%async_computation | async-start | bytes 4194304 | tf_op jit(solution)/shard_map/all_to_all | solution.py:45
  67.6 40.3 %while.42 = (s32[]{:T(128)}, s32[]{:T(128)}, s32[16]{0:T(128)S(1)}, s32[16]{0:T(128)S(1)}, s32[]{:T(128)}, /*index=5*/s32[]{:T(128)}, s32[]{:T(128)}) while((s32[]{:T(128)}, s32[]{:T(128)}, s32[16]{0:T(128)S(1)}, s32[16]{0:T(128)S(1)}, s32[]{:T(128)}, /*index=5*/s32[]{:T(128)}, s32[]{:T(128)}) %tuple.72), condition=%wide.region_2.3_spmd.clone, body=%wide.region_1.2_spmd.clone.sunk | while | flops 70 | bytes 273 | solution.py:58
  108.0 8.6 %all-to-all-done = bf16[128,16,512]{0,2,1:T(8,128)(2,1)S(1)} async-done(((bf16[128,16,512]{0,2,1:T(8,128)(2,1)}), bf16[128,16,512]{0,2,1:T(8,128)(2,1)S(1)}, u32[]{:S(2)}, u32[]{:S(2)}) %all-to-all-start) | async-done | bytes 2097184 | tf_op jit(solution)/shard_map/all_to_all | solution.py:45
  116.6 1.3 copy-done.7
  118.0 2.9 copy.52
  120.8 2.0 fusion.48
  122.9 56.6 %all-reduce.4 = bf16[2048,256]{1,0:T(8,128)(2,1)} all-reduce(f32[2048,256]{1,0:T(8,128)} %fusion.48), channel_id=1, replica_groups=mesh['dp'=4,'seq'=16,'tensor'=8] {'seq'}, use_global_device_ids=true, to_apply=%region_0.0 | all-reduce | flops 524288 | bytes 3145728 | tf_op jit(solution)/shard_map/psum | solution.py:47
  179.4 2.2 squeeze.41
  181.6 3.2 fusion.47
  184.8 1.8 copy.71
  186.7 39.9 %while.43 = (s32[]{:T(128)}, f32[2048,128]{1,0:T(8,128)}, f32[2048,128]{1,0:T(8,128)}, bf16[2,128,4,128]{3,1,2,0:T(8,128)(2,1)}, f32[2,128,4,128]{3,1,2,0:T(8,12...) while((s32[]{:T(128)}, f32[2048,128]{1,0:T(8,128)}, ...), condition=%wide.region_7.8_spmd.clone, body=%wide.region_3.7_spmd.clone.sunk | while | flops 1626342912 | bytes 79985504 | solution.py:88
  186.7 0.7 fusion.89
  187.7 1.9 fusion.91
  189.6 1.9 copy-done.2
  192.2 0.9 constant_dynamic-slice_fusion.3
  193.2 1.8 multiply_reduce_fusion.2
  195.1 4.5 %fusion.93 = bf16[4,128,2048]{2,1,0:T(8,128)(2,1)} fusion(f32[4,128]{1,0:T(4,128)S(1)} %bitcast.171, f32[4,128,2048]{2,1,0:T(8,128)} %copy-done.2, f32[4,128]{1,0:T(4,128)} %copy-done.11, bf16[2048,128]{0,1:T(8,128)(2,1)} %get-tuple-element.417, bf16[1,128,4,128]{1,3,2,0:T(8,128)(2,1)S(1)} %constant_dynamic-slice_fusion.3), kind=kOutput, calls=%fused_computation.9.clone.1 | convolution fusion | flops 273678336 | bytes 6950912 | tf_op jit(solution)/shard_map/while/body/eval_jaxpr/while/body/eval_jaxpr/thd,jd->htj/dot_general | solution.py:22
  199.6 3.5 fusion.94
  203.2 0.7 fusion.96
  203.9 1.0 fusion.95
  205.0 0.9 copy-done.4
  206.6 0.7 fusion.89
  207.5 1.9 fusion.91
  209.4 1.9 copy-done.2
  212.0 0.9 constant_dynamic-slice_fusion.3
  213.1 1.8 multiply_reduce_fusion.2
  214.9 4.5 %fusion.93 = bf16[4,128,2048]{2,1,0:T(8,128)(2,1)} fusion(f32[4,128]{1,0:T(4,128)S(1)} %bitcast.171, f32[4,128,2048]{2,1,0:T(8,128)} %copy-done.2, f32[4,128]{1,0:T(4,128)} %copy-done.11, bf16[2048,128]{0,1:T(8,128)(2,1)} %get-tuple-element.417, bf16[1,128,4,128]{1,3,2,0:T(8,128)(2,1)S(1)} %constant_dynamic-slice_fusion.3), kind=kOutput, calls=%fused_computation.9.clone.1 | convolution fusion | flops 273678336 | bytes 6950912 | tf_op jit(solution)/shard_map/while/body/eval_jaxpr/while/body/eval_jaxpr/thd,jd->htj/dot_general | solution.py:22
  219.4 3.8 fusion.94
  223.2 0.7 fusion.96
  224.0 1.0 fusion.95
  225.0 0.9 copy-done.4
  226.6 1.6 copy.61
  228.2 1.4 copy.60
  229.7 1.1 pad_maximum_fusion
  231.0 119.1 %all-reduce.3.cloned.1.call-done = bf16[2048,256]{0,1:T(8,128)(2,1)} async-done(((bf16[2048,256]{0,1:T(8,128)(2,1)}), bf16[2048,256]{0,1:T(8,128)(2,1)}) %all-reduce.3.cloned.1.call-update) | async-done | bytes 1048592 | tf_op jit(solution)/shard_map/psum | solution.py:95
  350.1 2.7 fusion.37
  353.3 1.0 reshape.59
  354.3 1.2 copy.58
  355.4 0.9 reshape.58
  356.3 32.5 %all-gather.6.cloned.1.call-done = f32[2048,256]{0,1:T(8,128)} async-done(((f32[512,256]{0,1:T(8,128)}), f32[2048,256]{0,1:T(8,128)}) %all-gather.6.cloned.1.call-update) | async-done | bytes 2097168 | tf_op jit(solution)/shard_map/all_gather | solution.py:100
  388.8 2.7 reshape.60
  391.5 1.2 reduce_sum.27
  392.7 1.0 copy.62
  (92 shorter events, 13.8 us)
Async XLA Ops:
  7.2 113.7 %copy-start = (bf16[512,256]{1,0:T(8,128)(2,1)S(1)}, bf16[512,256]{1,0:T(8,128)(2,1)}, u32[]{:S(2)}) copy-start(bf16[512,256]{1,0:T(8,128)(2,1)} %param.11) | copy-start | bytes 786436
  7.2 60.4 %copy-start.12 = (s32[1,16]{1,0:T(1,128)S(1)}, s32[1,16]{1,0:T(1,128)}, u32[]{:S(2)}) copy-start(s32[1,16]{1,0:T(1,128)} %param.12) | copy-start | bytes 196
  7.2 48.2 %all-gather.4.cloned.1.call-start = ((), (), s32[]{:S(2)}) async-start(), calls=%async_computation.1 | async-start | bytes 2359296 | tf_op jit(solution)/shard_map/all_gather | solution.py:44
  55.4 61.3 %all-to-all-start = ((bf16[128,16,512]{0,2,1:T(8,128)(2,1)}), bf16[128,16,512]{0,2,1:T(8,128)(2,1)S(1)}, u32[]{:S(2)}, u32[]{:S(2)}) async-start(bf16[128,16,512]{0,2,1:T(8,128)(2,1)} %bitcast.165), calls=%async_computation | async-start | bytes 4194304 | tf_op jit(solution)/shard_map/all_to_all | solution.py:45
  67.6 282.6 %all-reduce.3.cloned.1.call-start = ((), (), s32[]{:S(2)}) async-start(), calls=%async_computation.2 | async-start | bytes 2097152 | tf_op jit(solution)/shard_map/psum | solution.py:95
  116.6 1.3 copy-start.7
  120.8 58.6 %copy-start.5 = (bf16[16,128,512]{2,1,0:T(8,128)(2,1)}, bf16[16,128,512]{2,1,0:T(8,128)(2,1)S(1)}, u32[]{:S(2)}) copy-start(bf16[16,128,512]{2,1,0:T(8,128)(2,1)S(1)} %copy.52) | copy-start | bytes 6291460
  189.5 2.0 copy-start.2
  189.5 2.6 copy-start.11
  199.6 3.6 copy-start.1
  199.6 3.6 copy-start.8
  199.6 4.3 %copy-start.3 = (f32[2048,128]{1,0:T(8,128)S(1)}, f32[2048,128]{1,0:T(8,128)}, u32[]{:S(2)}) copy-start(f32[2048,128]{1,0:T(8,128)} %get-tuple-element.397) | copy-start | bytes 3145732 | tf_op jit(solution)/shard_map/while/body/eval_jaxpr/while
  203.9 2.0 copy-start.9
  204.9 1.0 copy-start.4
  209.4 2.0 copy-start.2
  209.4 2.6 copy-start.11
  219.4 3.8 copy-start.1
  219.4 3.8 copy-start.8
  219.4 4.5 %copy-start.3 = (f32[2048,128]{1,0:T(8,128)S(1)}, f32[2048,128]{1,0:T(8,128)}, u32[]{:S(2)}) copy-start(f32[2048,128]{1,0:T(8,128)} %get-tuple-element.397) | copy-start | bytes 3145732 | tf_op jit(solution)/shard_map/while/body/eval_jaxpr/while
  224.0 2.0 copy-start.9
  225.0 1.0 copy-start.4
  226.6 123.5 %copy-start.6 = (bf16[16,128,512]{2,1,0:T(8,128)(2,1)S(1)}, bf16[16,128,512]{2,1,0:T(8,128)(2,1)}, u32[]{:S(2)}) copy-start(bf16[16,128,512]{2,1,0:T(8,128)(2,1)} %copy-done.5) | copy-start | bytes 6291460
  230.8 122.1 %copy-start.10 = (f32[2,128,4,128]{3,1,2,0:T(8,128)S(1)}, f32[2,128,4,128]{3,1,2,0:T(8,128)}, u32[]{:S(2)}) copy-start(f32[2,128,4,128]{3,1,2,0:T(8,128)} %get-tuple-element.111) | copy-start | bytes 1572868
  230.8 158.0 %all-gather.6.cloned.1.call-start = ((), (), s32[]{:S(2)}) async-start(), calls=%async_computation.3 | async-start | bytes 2621440 | tf_op jit(solution)/shard_map/all_gather | solution.py:100
Sparse Core Ops, SparseCore 0:
  10.7 44.6 all-gather.3
  230.9 119.1 all-reduce.2
  353.0 35.7 all-gather.5
